TPU v7x, 32 devices: a whole 2x2x4 slice. The times are simulated.
32 devices in a mesh: sec: 2 (over x), blk: 8 (over z, y), mp: 2 (over core).
Axes of the slice: x: 2, y: 2, z: 4, core: 2. Of those that a mesh axis runs over, the one named last changes fastest.
Arguments:
- image_pooled: bfloat16 [1536, 1536], P('blk', ('sec', 'mp')), may hold values from -4 to 4
- text_pooled: bfloat16 [1536, 2048], P('blk', ('sec', 'mp')), may hold values from -4 to 4
- image_proj: bfloat16 [1536, 1152], P(('sec', 'mp')), may hold values from -0.15625 to 0.15625
- text_proj: bfloat16 [2048, 1152], P(('sec', 'mp')), may hold values from -0.125 to 0.125
- natural_log_multiplier: float32 [1], replicated, may hold values from 1.4 to 2.3
- logit_bias: float32 [1], replicated, may hold values from -2 to -0.5
- match_cluster_labels: int32 [1536], P('blk'), may hold values from 0 to 1535
Outputs:
- pair_loss: float32 [2, 1536], P('sec', 'blk')
- image_grad: bfloat16 [1536, 1536], P('blk', ('sec', 'mp'))
- text_grad: bfloat16 [1536, 2048], P('blk', ('sec', 'mp'))
All inputs are finite; a program needn't handle non-finite values.
Results may differ from a plain program's by a relative error of at most 0.0065.
Values may be sent and summed in bfloat16 or wider, within the bound.
No kernel may reach another device: no remote copies, remote signals or barrier semaphores. Data moves between devices by JAX's collectives and lax.ppermute only.
A program may use at most 128 MiB of HBM per device.

v0:
```python
import jax
import jax.numpy as jnp
from jax import lax
from jax.sharding import PartitionSpec as P


def unit_rows(embedding):
    row_norm = jnp.sqrt(jnp.sum(embedding * embedding, axis=1, keepdims=True) + 1e-06)
    return (embedding / row_norm, row_norm)


def per_device(
    image_pooled,
    text_pooled,
    image_proj,
    text_proj,
    natural_log_multiplier,
    logit_bias,
    match_cluster_labels,
):
    part_image = jnp.dot(image_pooled, image_proj, preferred_element_type=jnp.float32)
    part_text = jnp.dot(text_pooled, text_proj, preferred_element_type=jnp.float32)
    stacked = jnp.stack([part_image, part_text])
    section = lax.axis_index("sec")
    both_sums = lax.psum(stacked, ("sec", "mp"))
    own_emb = lax.dynamic_index_in_dim(both_sums, section, 0, keepdims=False)
    other_emb = lax.dynamic_index_in_dim(both_sums, 1 - section, 0, keepdims=False)
    own_unit, own_norm = unit_rows(own_emb)
    resident_slice = own_unit.astype(jnp.bfloat16)
    other_unit, other_norm = unit_rows(other_emb)
    counterpart_slice = other_unit.astype(jnp.bfloat16)
    sharpness_factor = jnp.exp(natural_log_multiplier[0])
    shift_quantity = logit_bias[0]
    visit_rows = lax.all_gather(counterpart_slice, "blk", axis=0, tiled=True)
    visited_ids = lax.all_gather(match_cluster_labels, "blk", axis=0, tiled=True)
    agreement_scores_matrix = (
        sharpness_factor
        * lax.dot_general(
            resident_slice, visit_rows, (((1,), (1,)), ((), ())), preferred_element_type=jnp.float32
        )
        + shift_quantity
    )
    desired_polarity = jnp.where(
        match_cluster_labels[:, None] == visited_ids[None, :], 1.0, -1.0
    ).astype(jnp.float32)
    row_losses = jnp.sum(jax.nn.softplus(-desired_polarity * agreement_scores_matrix), axis=1)
    penalty_factor = (
        -sharpness_factor
        * desired_polarity
        * jax.nn.sigmoid(-desired_polarity * agreement_scores_matrix)
    ).astype(jnp.bfloat16)
    unit_grad = jnp.dot(penalty_factor, visit_rows, preferred_element_type=jnp.float32)
    unit_grad, row_losses = (unit_grad, row_losses)
    projection = jnp.sum(own_unit * unit_grad, axis=1, keepdims=True)
    own_demb = ((unit_grad - own_unit * projection) / own_norm).astype(jnp.bfloat16)
    both_grads = lax.all_gather(own_demb[None], "sec", axis=0, tiled=True)
    image_grad = lax.dot_general(
        both_grads[0], image_proj, (((1,), (1,)), ((), ())), preferred_element_type=jnp.float32
    ).astype(jnp.bfloat16)
    text_grad = lax.dot_general(
        both_grads[1], text_proj, (((1,), (1,)), ((), ())), preferred_element_type=jnp.float32
    ).astype(jnp.bfloat16)
    return (row_losses[None, :], image_grad, text_grad)


def solution(mesh):
    placed = (
        P("blk", ("sec", "mp")),
        P("blk", ("sec", "mp")),
        P(("sec", "mp"), None),
        P(("sec", "mp"), None),
        P(),
        P(),
        P("blk"),
    )
    return jax.shard_map(
        per_device,
        mesh=mesh,
        in_specs=placed,
        out_specs=(P("sec", "blk"), P("blk", ("sec", "mp")), P("blk", ("sec", "mp"))),
        check_vma=False,
    )
```

profile of v0, /device:TPU:0, one launch (start us, length us, event | category | flops | bytes accessed | tf_op | source)
XLA Modules:
  0.0 155.9 jit_solution(17890607806463199969)
XLA Ops:
  7.2 0.0 copy-start
  7.2 0.0 copy-start.4
  7.2 0.0 copy-start.2
  7.2 0.0 all-reduce.3.cloned.1.call-start
  7.2 1.2 copy-done
  8.4 1.4 convolution_bitcast_fusion
  9.8 0.0 copy-done.4
  9.8 0.0 copy-done.2
  9.8 0.4 convolution_bitcast_fusion.1
  10.2 1.3 pad_maximum_fusion
  11.6 0.0 all-reduce.3.cloned.1.call-update
  11.6 0.0 all-gather.3.cloned.1.call-start
  11.6 48.8 %all-reduce.3.cloned.1.call-done = f32[2,192,1152]{2,1,0:T(8,128)} async-done(((f32[2,192,1152]{2,1,0:T(8,128)}), f32[2,192,1152]{2,1,0:T(8,128)}) %all-reduce.3.cloned.1.call-update) | async-done | bytes 1769488 | tf_op jit(solution)/shard_map/psum | solution.py:25
  60.5 1.8 %fusion.7 = (f32[192]{0:T(256)S(1)}, f32[192]{0:T(256)S(1)}) fusion(f32[2,192,1152]{2,1,0:T(8,128)} %all-reduce.3.cloned.1.call-done, s32[]{:T(128)S(6)} %select_n.16, s32[]{:T(128)S(6)} %select_n.17), kind=kLoop, calls=%fused_computation.20 | loop fusion | flops 884352 | bytes 1771016 | tf_op jit(solution)/shard_map/reduce_sum | solution.py:8
  62.2 0.0 copy-start.7
  62.3 0.0 copy-start.5
  62.3 0.2 copy-done.1
  62.5 0.9 fusion.6
  63.4 0.0 all-gather.3.cloned.1.call-update
  64.7 0.0 copy-done.7
  64.8 0.6 dynamic-slice
  66.0 0.0 copy-done.5
  66.0 0.3 dynamic-update-slice
  66.3 12.1 %all-reduce = s32[1536]{0:T(1024)S(1)} all-reduce(s32[1536]{0:T(1024)S(1)} %dynamic-update-slice), channel_id=1, replica_groups=mesh['sec'=2,'blk'=8,'mp'=2] {'blk'}, use_global_device_ids=true, to_apply=%add | all-reduce | flops 1536 | bytes 12288
  78.4 50.5 %all-gather.3.cloned.1.call-done = bf16[1536,1152]{1,0:T(8,128)(2,1)} async-done(((bf16[192,1152]{1,0:T(8,128)(2,1)}), bf16[1536,1152]{1,0:T(8,128)(2,1)}) %all-gather.3.cloned.1.call-update) | async-done | bytes 3538960 | tf_op jit(solution)/shard_map/all_gather | solution.py:34
  128.9 4.7 %fusion.4 = (f32[192]{0:T(256)}, f32[192,1536]{1,0:T(8,128)S(1)}) fusion(f32[]{:T(128)} %bitcast.37, bf16[1536,1152]{1,0:T(8,128)(2,1)} %all-gather.3.cloned.1.call-done, f32[192]{0:T(256)S(1)} %add_sqrt_fusion.1, f32[2,192,1152]{2,1,0:T(8,128)S(1)} %copy-done.1, s32[]{:T(128)S(6)} %select_n.16, f32[]{:T(128)} %bitcast.1, s32[1536]{0:T(1024)S(1)} %all-reduce, ...), kind=kOutput, calls=%fused_computation.11 | convolution fusion | flops 683753280 | bytes 5614348 | tf_op jit(solution)/shard_map/dot_general | solution.py:38
  133.6 1.1 multiply_reduce_fusion
  134.7 0.2 divide_convert_fusion
  135.0 0.0 copy-start.3
  135.0 11.7 %all-gather = bf16[384,1152]{1,0:T(8,128)(2,1)S(1)} all-gather(bf16[192,1152]{1,0:T(8,128)(2,1)S(1)} %divide_convert_fusion), channel_id=2, replica_groups=mesh['sec'=2,'blk'=8,'mp'=2] {'sec'}, dimensions={0}, use_global_device_ids=true | all-gather | bytes 1327104 | tf_op jit(solution)/shard_map/all_gather | solution.py:56
  146.7 1.1 convolution_convert_fusion.1
  147.8 1.2 convolution_convert_fusion
  (7 shorter events, 0.0 us)
Async XLA Ops:
  7.2 1.3 copy-start
  7.2 2.6 %copy-start.4 = (bf16[192,384]{1,0:T(8,128)(2,1)S(1)}, bf16[192,384]{1,0:T(8,128)(2,1)}, u32[]{:S(2)}) copy-start(bf16[192,384]{1,0:T(8,128)(2,1)} %param.7) | copy-start | bytes 442372
  7.2 2.6 %copy-start.2 = (bf16[384,1152]{1,0:T(8,128)(2,1)S(1)}, bf16[384,1152]{1,0:T(8,128)(2,1)}, u32[]{:S(2)}) copy-start(bf16[384,1152]{1,0:T(8,128)(2,1)} %param.9) | copy-start | bytes 2654212
  7.2 53.3 %all-reduce.3.cloned.1.call-start = ((), (), s32[]{:S(2)}) async-start(), calls=%async_computation | async-start | bytes 3538944 | tf_op jit(solution)/shard_map/psum | solution.py:25
  11.6 117.3 %all-gather.3.cloned.1.call-start = ((), (), s32[]{:S(2)}) async-start(), calls=%async_computation.1 | async-start | bytes 3981312 | tf_op jit(solution)/shard_map/all_gather | solution.py:34
  60.5 2.0 %copy-start.1 = (f32[2,192,1152]{2,1,0:T(8,128)S(1)}, f32[2,192,1152]{2,1,0:T(8,128)}, u32[]{:S(2)}) copy-start(f32[2,192,1152]{2,1,0:T(8,128)} %all-reduce.3.cloned.1.call-done) | copy-start | bytes 5308420
  62.2 2.5 %copy-start.7 = (u32[32]{0:T(128)S(1)}, u32[32]{0:T(128)}, u32[]{:S(2)}) copy-start(u32[32]{0:T(128)} %constant.31) | copy-start | bytes 388
  62.3 3.8 %copy-start.5 = (s32[192]{0:T(256)S(1)}, s32[192]{0:T(256)}, u32[]{:S(2)}) copy-start(s32[192]{0:T(256)} %param.13) | copy-start | bytes 2308
  128.9 4.7 %copy-start.6 = (bf16[1536,1152]{1,0:T(8,128)(2,1)S(1)}, bf16[1536,1152]{1,0:T(8,128)(2,1)}, u32[]{:S(2)}) copy-start(bf16[1536,1152]{1,0:T(8,128)(2,1)} %all-gather.3.cloned.1.call-done) | copy-start | bytes 10616836
  135.0 11.8 %copy-start.3 = (bf16[384,1152]{1,0:T(8,128)(2,1)S(1)}, bf16[384,1152]{1,0:T(8,128)(2,1)}, u32[]{:S(2)}) copy-start(bf16[384,1152]{1,0:T(8,128)(2,1)} %param.9) | copy-start | bytes 2654212
Sparse Core Ops, SparseCore 0:
  11.7 48.7 all-reduce.2
  63.5 65.3 all-gather.2
where the time goes:
time: 156 us
  waiting for transfers between devices  99.4 us (64%)
  blocking collectives  23.8 us (15%)
  between operations  16.2 us (10%)
  matrix products  9.9 us (6%)
  other arithmetic  4.2 us (3%)
  local copies, waits for them, and re-layouts  2.31 us (1%)
    all_gather x1, waiting for transfers between devices, per_device(): visit_rows = lax.all_gather(counterpart_slice, 'blk', axis=0, tiled=True)  50.5 us
    psum x1, waiting for transfers between devices, per_device(): both_sums = lax.psum(stacked, ('sec', 'mp'))  48.8 us
    unnamed x1, blocking collectives  12.1 us
    all_gather x1, blocking collectives, per_device(): both_grads = lax.all_gather(own_demb[None], 'sec', axis=0, tiled=True)  11.7 us
    dot_general x1, matrix products, per_device(): lax.dot_general(resident_slice, visit_rows, (((1,), (1,)), ((), ())), pre...  4.68 us
  transfers between devices with their start and end apart: 2, of which 2 were waited for; matrix products, arithmetic and copies ran while one was open for 1% of the time, Pallas kernels for 0%

commit v1 on v0

--- a/solution.py
+++ b/solution.py
@@ -31,7 +31,27 @@
     counterpart_slice = other_unit.astype(jnp.bfloat16)
     sharpness_factor = jnp.exp(natural_log_multiplier[0])
     shift_quantity = logit_bias[0]
-    visit_rows = lax.all_gather(counterpart_slice, "blk", axis=0, tiled=True)
+    size, index, span = (lax.axis_size("blk"), lax.axis_index("blk"), counterpart_slice.shape[0])
+    right = [(i, (i + 1) % size) for i in range(size)]
+    backward = [(i, (i - 1) % size) for i in range(size)]
+    result = jnp.zeros(
+        (*counterpart_slice.shape[:0], size * span, *counterpart_slice.shape[0 + 1 :]),
+        counterpart_slice.dtype,
+    )
+    result = lax.dynamic_update_slice_in_dim(result, counterpart_slice, index * span, axis=0)
+    from_left = from_right = counterpart_slice
+    halfway = size // 2
+    for hop in range(1, halfway + 1):
+        from_left = lax.ppermute(from_left, "blk", right)
+        result = lax.dynamic_update_slice_in_dim(
+            result, from_left, (index - hop) % size * span, axis=0
+        )
+        if hop < size - halfway:
+            from_right = lax.ppermute(from_right, "blk", backward)
+            result = lax.dynamic_update_slice_in_dim(
+                result, from_right, (index + hop) % size * span, axis=0
+            )
+    visit_rows = result
     visited_ids = lax.all_gather(match_cluster_labels, "blk", axis=0, tiled=True)
     agreement_scores_matrix = (
         sharpness_factor

time: 156 us -> 174 us (1.12)
  waiting for transfers between devices: 99.4 us -> 82.2 us
  starting transfers between devices: 0.08 us -> 16.7 us
  local copies, waits for them, and re-layouts: 2.31 us -> 10.9 us
  blocking collectives: 23.8 us -> 31.3 us
  matrix products: 9.9 us -> 11.7 us
    all_gather x1 -> x0, waiting for transfers between devices: 50.5 us -> none  [per_device(): visit_rows = lax.all_gather(counterpart_slice, 'blk', axis=0, tiled=True)]
    ppermute x0 -> x7, waiting for transfers between devices: none -> 33.3 us  [the longest x4 33.3 us: per_device(): from_left = lax.ppermute(from_left, 'blk', right)]
    ppermute x0 -> x7, starting transfers between devices: none -> 16.7 us  [the longest x3 9.67 us: per_device(): from_right = lax.ppermute(from_right, 'blk', backward)]
    unnamed x1, blocking collectives: 12.1 us -> 22.2 us
    dynamic_update_slice x0 -> x7, local copies, waits for them, and re-layouts: none -> 6.66 us  [the longest x4 4.24 us: per_device(): lax.dynamic_update_slice_in_dim(result, from_left, (index - hop) % size *...]
    all_gather x1, blocking collectives: 11.7 us -> 9.11 us  [per_device(): both_grads = lax.all_gather(own_demb[None], 'sec', axis=0, tiled=True)]
    broadcast_in_dim x0 -> x1, local copies, waits for them, and re-layouts: none -> 2.01 us  [per_device(): jnp.zeros((*counterpart_slice.shape[:0], size * span, *counterpart_slice....]
    dot_general x1, matrix products: 1.12 us -> 3.12 us  [per_device(): jnp.dot(penalty_factor, visit_rows, preferred_element_type=jnp.float32)]
  transfers between devices with their start and end apart: 2 -> 8, of which waited for: 2 -> 4; matrix products, arithmetic and copies ran while one was open for 1% -> 4% of each run, Pallas kernels for 0% -> 0%
where the time goes in v1:
time: 174 us; the launch traced here: 173 us
  waiting for transfers between devices  82.2 us (47%)
  blocking collectives  31.3 us (18%)
  starting transfers between devices  16.7 us (10%)
  between operations  16.2 us (9%)
  matrix products  11.7 us (7%)
  local copies, waits for them, and re-layouts  10.9 us (6%)
  other arithmetic  4.28 us (2%)
    psum x1, waiting for transfers between devices, per_device(): both_sums = lax.psum(stacked, ('sec', 'mp'))  48.9 us
    ppermute x4, waiting for transfers between devices, per_device(): from_left = lax.ppermute(from_left, 'blk', right)  33.3 us
    unnamed x1, blocking collectives  22.2 us
    ppermute x3, starting transfers between devices, per_device(): from_right = lax.ppermute(from_right, 'blk', backward)  9.67 us
    all_gather x1, blocking collectives, per_device(): both_grads = lax.all_gather(own_demb[None], 'sec', axis=0, tiled=True)  9.11 us
    ppermute x4, starting transfers between devices, per_device(): from_left = lax.ppermute(from_left, 'blk', right)  7.03 us
    dot_general x1, matrix products, per_device(): lax.dot_general(resident_slice, visit_rows, (((1,), (1,)), ((), ())), pre...  4.53 us
    dynamic_update_slice x4, local copies, waits for them, and re-layouts, per_device(): lax.dynamic_update_slice_in_dim(result, from_left, (index - hop) % size *...  4.24 us
  transfers between devices with their start and end apart: 8, of which 4 were waited for; matrix products, arithmetic and copies ran while one was open for 4% of the time, Pallas kernels for 0%

profile of v1, /device:TPU:0, one launch (start us, length us, event | category | flops | bytes accessed | tf_op | source)
XLA Modules:
  0.0 173.3 jit_solution(9222464023707049804)
XLA Ops:
  7.2 1.2 copy-done
  8.4 1.4 convolution_bitcast_fusion
  9.8 0.4 convolution_bitcast_fusion.1
  10.2 1.4 pad_maximum_fusion
  11.6 48.9 %all-reduce.3.cloned.1.call-done = f32[2,192,1152]{2,1,0:T(8,128)} async-done(((f32[2,192,1152]{2,1,0:T(8,128)}), f32[2,192,1152]{2,1,0:T(8,128)}) %all-reduce.3.cloned.1.call-update) | async-done | bytes 1769488 | tf_op jit(solution)/shard_map/psum | solution.py:25
  60.5 1.6 fusion.7
  62.2 2.0 %broadcast_in_dim.24 = bf16[1536,1152]{1,0:T(8,128)(2,1)} broadcast(bf16[]{:T(256)} %constant.75.clone.1), dimensions={} | broadcast | bytes 3538946 | tf_op jit(solution)/shard_map/broadcast_in_dim | solution.py:37
  64.3 1.1 constant_dynamic-update-slice_fusion.7
  65.3 1.5 collective-permute-start
  66.8 3.2 %collective-permute-start.1 = (bf16[192,1152]{1,0:T(8,128)(2,1)}, bf16[192,1152]{1,0:T(8,128)(2,1)S(1)}, u32[]{:S(2)}, u32[]{:S(2)}) collective-permute-start(bf16[192,1152]{1,0:T(8,128)(2,1)} %get-tuple-element.6), channel_id=1, source_target_pairs={{0,14},{2,0},{4,2},{6,4},{8,6},{10,8},{12,10},{14,12},{1,15},{3,1}... | collective-permute-start | bytes 1327112 | tf_op jit(solution)/shard_map/ppermute | solution.py:50
  71.4 0.6 dynamic-slice
  73.0 22.2 %all-reduce = s32[1536]{0:T(1024)S(1)} all-reduce(s32[1536]{0:T(1024)S(1)} %dynamic-update-slice), channel_id=1, replica_groups=mesh['sec'=2,'blk'=8,'mp'=2] {'blk'}, use_global_device_ids=true, to_apply=%add | all-reduce | flops 1536 | bytes 12288
  95.2 0.7 collective-permute-start.2
  95.9 4.1 %collective-permute-start.3 = (bf16[192,1152]{1,0:T(8,128)(2,1)S(1)}, bf16[192,1152]{1,0:T(8,128)(2,1)S(1)}, u32[]{:S(2)}, u32[]{:S(2)}) collective-permute-start(bf16[192,1152]{1,0:T(8,128)(2,1)S(1)} %collective-permute-done.1), channel_id=1, source_target_pairs={{0,14},{2,0},{4,2},{6,4},{8,6},{10,8},{12,10},{14,12},{1,15},{3,1}... | collective-permute-start | bytes 1327112 | tf_op jit(solution)/shard_map/ppermute | solution.py:50
  100.0 1.8 %constant_dynamic-update-slice_fusion.6 = bf16[1536,1152]{1,0:T(8,128)(2,1)} fusion(bf16[1536,1152]{1,0:T(8,128)(2,1)} %get-tuple-element.5, bf16[192,1152]{1,0:T(8,128)(2,1)} %collective-permute-done, s32[]{:T(128)S(6)} %select_n.75), kind=kLoop, calls=%fused_computation.38 | loop fusion | bytes 884740 | tf_op jit(solution)/shard_map/dynamic_update_slice | solution.py:46
  101.8 0.8 constant_dynamic-update-slice_fusion.5
  102.6 10.6 %collective-permute-done.2 = bf16[192,1152]{1,0:T(8,128)(2,1)S(1)} collective-permute-done((bf16[192,1152]{1,0:T(8,128)(2,1)}, bf16[192,1152]{1,0:T(8,128)(2,1)S(1)}, u32[]{:S(2)}, u32[]{:S(2)}) %collective-permute-start.2) | collective-permute-done | bytes 442400 | tf_op jit(solution)/shard_map/ppermute | solution.py:45
  113.2 2.4 %collective-permute-start.4 = (bf16[192,1152]{1,0:T(8,128)(2,1)S(1)}, bf16[192,1152]{1,0:T(8,128)(2,1)S(1)}, u32[]{:S(2)}, u32[]{:S(2)}) collective-permute-start(bf16[192,1152]{1,0:T(8,128)(2,1)S(1)} %collective-permute-done.2), channel_id=1, source_target_pairs={{0,2},{2,4},{4,6},{6,8},{8,10},{10,12},{12,14},{14,0},{1,3},{3,5},... | collective-permute-start | bytes 1327112 | tf_op jit(solution)/shard_map/ppermute | solution.py:45
  115.6 2.3 %collective-permute-start.5 = (bf16[192,1152]{1,0:T(8,128)(2,1)S(1)}, bf16[192,1152]{1,0:T(8,128)(2,1)S(1)}, u32[]{:S(2)}, u32[]{:S(2)}) collective-permute-start(bf16[192,1152]{1,0:T(8,128)(2,1)S(1)} %collective-permute-done.3), channel_id=1, source_target_pairs={{0,14},{2,0},{4,2},{6,4},{8,6},{10,8},{12,10},{14,12},{1,15},{3,1}... | collective-permute-start | bytes 1327112 | tf_op jit(solution)/shard_map/ppermute | solution.py:50
  117.9 0.8 constant_dynamic-update-slice_fusion.4
  118.8 0.8 constant_dynamic-update-slice_fusion.3
  119.6 13.0 %collective-permute-done.4 = bf16[192,1152]{1,0:T(8,128)(2,1)S(1)} collective-permute-done((bf16[192,1152]{1,0:T(8,128)(2,1)S(1)}, bf16[192,1152]{1,0:T(8,128)(2,1)S(1)}, u32[]{:S(2)}, u32[]{:S(2)}) %collective-permute-start.4) | collective-permute-done | bytes 442400 | tf_op jit(solution)/shard_map/ppermute | solution.py:45
  132.5 2.5 %collective-permute-start.6 = (bf16[192,1152]{1,0:T(8,128)(2,1)S(1)}, bf16[192,1152]{1,0:T(8,128)(2,1)S(1)}, u32[]{:S(2)}, u32[]{:S(2)}) collective-permute-start(bf16[192,1152]{1,0:T(8,128)(2,1)S(1)} %collective-permute-done.4), channel_id=1, source_target_pairs={{0,2},{2,4},{4,6},{6,8},{8,10},{10,12},{12,14},{14,0},{1,3},{3,5},... | collective-permute-start | bytes 1327112 | tf_op jit(solution)/shard_map/ppermute | solution.py:45
  135.0 0.8 constant_dynamic-update-slice_fusion.2
  135.8 0.8 constant_dynamic-update-slice_fusion.1
  136.6 9.7 %collective-permute-done.6 = bf16[192,1152]{1,0:T(8,128)(2,1)S(1)} collective-permute-done((bf16[192,1152]{1,0:T(8,128)(2,1)S(1)}, bf16[192,1152]{1,0:T(8,128)(2,1)S(1)}, u32[]{:S(2)}, u32[]{:S(2)}) %collective-permute-start.6) | collective-permute-done | bytes 442400 | tf_op jit(solution)/shard_map/ppermute | solution.py:45
  146.3 0.8 constant_dynamic-update-slice_fusion
  147.1 4.5 %fusion.4 = (f32[192]{0:T(256)}, f32[192,1536]{1,0:T(8,128)S(1)}) fusion(f32[]{:T(128)} %bitcast.38, bf16[1536,1152]{1,0:T(8,128)(2,1)} %constant_dynamic-update-slice_fusion, f32[192]{0:T(256)S(1)} %add_sqrt_fusion.1, f32[2,192,1152]{2,1,0:T(8,128)S(1)} %copy-done.1, s32[]{:T(128)S(6)} %select_n.71, f32[]{:T(128)} %bitcast.1, s32[1536]{0:T(1024)S(1)} %all-reduce, ...), kind=kOutput, calls=%fused_computation.11 | convolution fusion | flops 683753280 | bytes 5614348 | tf_op jit(solution)/shard_map/dot_general | solution.py:58
  151.7 3.1 %multiply_reduce_fusion = (f32[192]{0:T(256)S(1)}, f32[192,1152]{1,0:T(8,128)S(1)}) fusion(f32[192]{0:T(256)S(1)} %add_sqrt_fusion.1, f32[2,192,1152]{2,1,0:T(8,128)S(1)} %copy-done.1, s32[]{:T(128)S(6)} %select_n.71, bf16[1536,1152]{1,0:T(8,128)(2,1)} %constant_dynamic-update-slice_fusion, f32[192,1536]{1,0:T(8,128)S(1)} %get-tuple-element.8, ...), kind=kOutput, calls=%fused_computation.22 | convolution fusion | flops 682499904 | bytes 6496520 | tf_op jit(solution)/shard_map/dot_general | solution.py:72
  155.0 9.1 %all-gather = bf16[384,1152]{1,0:T(8,128)(2,1)S(1)} all-gather(bf16[192,1152]{1,0:T(8,128)(2,1)S(1)} %divide_convert_fusion), channel_id=2, replica_groups=mesh['sec'=2,'blk'=8,'mp'=2] {'sec'}, dimensions={0}, use_global_device_ids=true | all-gather | bytes 1327104 | tf_op jit(solution)/shard_map/all_gather | solution.py:76
  164.1 1.2 convolution_convert_fusion
  165.4 1.1 convolution_convert_fusion.1
  (24 shorter events, 0.7 us)
Async XLA Ops:
  7.2 1.3 copy-start
  7.2 2.6 %copy-start.4 = (bf16[192,384]{1,0:T(8,128)(2,1)S(1)}, bf16[192,384]{1,0:T(8,128)(2,1)}, u32[]{:S(2)}) copy-start(bf16[192,384]{1,0:T(8,128)(2,1)} %param.7) | copy-start | bytes 442372
  7.2 2.6 %copy-start.2 = (bf16[384,1152]{1,0:T(8,128)(2,1)S(1)}, bf16[384,1152]{1,0:T(8,128)(2,1)}, u32[]{:S(2)}) copy-start(bf16[384,1152]{1,0:T(8,128)(2,1)} %param.9) | copy-start | bytes 2654212
  7.2 53.3 %all-reduce.3.cloned.1.call-start = ((), (), s32[]{:S(2)}) async-start(), calls=%async_computation | async-start | bytes 3538944 | tf_op jit(solution)/shard_map/psum | solution.py:25
  62.2 2.1 %copy-start.1 = (f32[2,192,1152]{2,1,0:T(8,128)S(1)}, f32[2,192,1152]{2,1,0:T(8,128)}, u32[]{:S(2)}) copy-start(f32[2,192,1152]{2,1,0:T(8,128)} %all-reduce.3.cloned.1.call-done) | copy-start | bytes 5308420
  64.3 7.1 %copy-start.6 = (u32[32]{0:T(128)S(1)}, u32[32]{0:T(128)}, u32[]{:S(2)}) copy-start(u32[32]{0:T(128)} %constant.89) | copy-start | bytes 388
  64.3 8.4 %copy-start.5 = (s32[192]{0:T(256)S(1)}, s32[192]{0:T(256)}, u32[]{:S(2)}) copy-start(s32[192]{0:T(256)} %param.13) | copy-start | bytes 2308
  65.3 29.9 %collective-permute-start = (bf16[192,1152]{1,0:T(8,128)(2,1)}, bf16[192,1152]{1,0:T(8,128)(2,1)}, u32[]{:S(2)}, u32[]{:S(2)}) collective-permute-start(bf16[192,1152]{1,0:T(8,128)(2,1)} %get-tuple-element.6), channel_id=1, source_target_pairs={{0,2},{2,4},{4,6},{6,8},{8,10},{10,12},{12,14},{14,0},{1,3},{3,5},... | collective-permute-start | bytes 1327112 | tf_op jit(solution)/shard_map/ppermute | solution.py:45
  66.8 29.1 %collective-permute-start.1 = (bf16[192,1152]{1,0:T(8,128)(2,1)}, bf16[192,1152]{1,0:T(8,128)(2,1)S(1)}, u32[]{:S(2)}, u32[]{:S(2)}) collective-permute-start(bf16[192,1152]{1,0:T(8,128)(2,1)} %get-tuple-element.6), channel_id=1, source_target_pairs={{0,14},{2,0},{4,2},{6,4},{8,6},{10,8},{12,10},{14,12},{1,15},{3,1}... | collective-permute-start | bytes 1327112 | tf_op jit(solution)/shard_map/ppermute | solution.py:50
  95.2 18.0 %collective-permute-start.2 = (bf16[192,1152]{1,0:T(8,128)(2,1)}, bf16[192,1152]{1,0:T(8,128)(2,1)S(1)}, u32[]{:S(2)}, u32[]{:S(2)}) collective-permute-start(bf16[192,1152]{1,0:T(8,128)(2,1)} %collective-permute-done), channel_id=1, source_target_pairs={{0,2},{2,4},{4,6},{6,8},{8,10},{10,12},{12,14},{14,0},{1,3},{3,5},... | collective-permute-start | bytes 1327112 | tf_op jit(solution)/shard_map/ppermute | solution.py:45
  95.9 19.7 %collective-permute-start.3 = (bf16[192,1152]{1,0:T(8,128)(2,1)S(1)}, bf16[192,1152]{1,0:T(8,128)(2,1)S(1)}, u32[]{:S(2)}, u32[]{:S(2)}) collective-permute-start(bf16[192,1152]{1,0:T(8,128)(2,1)S(1)} %collective-permute-done.1), channel_id=1, source_target_pairs={{0,14},{2,0},{4,2},{6,4},{8,6},{10,8},{12,10},{14,12},{1,15},{3,1}... | collective-permute-start | bytes 1327112 | tf_op jit(solution)/shard_map/ppermute | solution.py:50
  113.2 19.3 %collective-permute-start.4 = (bf16[192,1152]{1,0:T(8,128)(2,1)S(1)}, bf16[192,1152]{1,0:T(8,128)(2,1)S(1)}, u32[]{:S(2)}, u32[]{:S(2)}) collective-permute-start(bf16[192,1152]{1,0:T(8,128)(2,1)S(1)} %collective-permute-done.2), channel_id=1, source_target_pairs={{0,2},{2,4},{4,6},{6,8},{8,10},{10,12},{12,14},{14,0},{1,3},{3,5},... | collective-permute-start | bytes 1327112 | tf_op jit(solution)/shard_map/ppermute | solution.py:45
  115.6 20.2 %collective-permute-start.5 = (bf16[192,1152]{1,0:T(8,128)(2,1)S(1)}, bf16[192,1152]{1,0:T(8,128)(2,1)S(1)}, u32[]{:S(2)}, u32[]{:S(2)}) collective-permute-start(bf16[192,1152]{1,0:T(8,128)(2,1)S(1)} %collective-permute-done.3), channel_id=1, source_target_pairs={{0,14},{2,0},{4,2},{6,4},{8,6},{10,8},{12,10},{14,12},{1,15},{3,1}... | collective-permute-start | bytes 1327112 | tf_op jit(solution)/shard_map/ppermute | solution.py:50
  132.5 13.8 %collective-permute-start.6 = (bf16[192,1152]{1,0:T(8,128)(2,1)S(1)}, bf16[192,1152]{1,0:T(8,128)(2,1)S(1)}, u32[]{:S(2)}, u32[]{:S(2)}) collective-permute-start(bf16[192,1152]{1,0:T(8,128)(2,1)S(1)} %collective-permute-done.4), channel_id=1, source_target_pairs={{0,2},{2,4},{4,6},{6,8},{8,10},{10,12},{12,14},{14,0},{1,3},{3,5},... | collective-permute-start | bytes 1327112 | tf_op jit(solution)/shard_map/ppermute | solution.py:45
  155.0 10.4 %copy-start.3 = (bf16[384,1152]{1,0:T(8,128)(2,1)S(1)}, bf16[384,1152]{1,0:T(8,128)(2,1)}, u32[]{:S(2)}) copy-start(bf16[384,1152]{1,0:T(8,128)(2,1)} %param.9) | copy-start | bytes 2654212
Sparse Core Ops, SparseCore 0:
  11.7 48.7 all-reduce.2
